TPU v7x, 512 devices: a whole 4x4x16 slice. The times are simulated.
512 devices in a mesh: seq: 16 (over y, x), dp: 32 (over z, core).
Axes of the slice: x: 4, y: 4, z: 16, core: 2. Of those that a mesh axis runs over, the one named last changes fastest.
Arguments:
- queries: bfloat16 [32, 2048, 2048], P('dp', 'seq'), may hold values from -30 to 30
- key_states: bfloat16 [32, 2048, 2048], P('dp', 'seq'), may hold values from -4.5 to 4.5
- value_states: bfloat16 [32, 2048, 2048], P('dp', 'seq'), may hold values from -6 to 6
- grad_out: bfloat16 [32, 2048, 2048], P('dp', 'seq'), may hold values from -18 to 18
- out_weight: bfloat16 [2048, 2048], P('dp'), may hold values from -0.125 to 0.125
- block_lists: int32 [16, 16, 8], P('seq'), may hold values from 0 to 15, as said below
- block_counts: int32 [16, 16], P('seq'), may hold values from 1 to 8, as said below
Outputs:
- query_grad: bfloat16 [32, 2048, 2048], P('dp', 'seq')
- key_grad: bfloat16 [32, 2048, 2048], P('dp', 'seq')
- value_grad: bfloat16 [32, 2048, 2048], P('dp', 'seq')
Inputs may be any that keep to these rules, and one draw needn't show every extreme that they name: The entries of one row block_lists[h, i, :] are distinct. `block_counts`: the counts of one head sum to at most 64; in every draw some head sums to exactly 64 and some query block uses all 8 entries.
All inputs are finite; a program needn't handle non-finite values.
Results may differ from a plain program's by a relative error of at most 0.0093.
Values may be sent and summed in bfloat16 or wider, within the bound.
A program may use at most 64 MiB of HBM per device.

v0:
```python
import jax
import jax.numpy as jnp
from jax import lax
from jax.sharding import PartitionSpec as P

HD = 128


def whole_rows(query_blocks, key_blocks, value_blocks, grad_blocks, lists_head, counts_head):
    nblocks, block_rows, head_width = query_blocks.shape
    kslots = lists_head.shape[1]
    group = 4
    score_scale = head_width ** (-0.5)

    def scan_step(running, block_slot):
        key_sum, value_sum = running
        query_group, grad_group, lists_group, counts_group = block_slot
        key_sets = key_blocks[lists_group]
        value_sets = value_blocks[lists_group]
        live_slots = jnp.arange(kslots, dtype=jnp.int32)[None, :] < counts_group[:, None]
        live_mask = live_slots[:, None, :, None]
        scores = (
            jnp.einsum("gqd,gjkd->gqjk", query_group, key_sets, preferred_element_type=jnp.float32)
            * score_scale
        )
        scores = jnp.where(live_mask, scores, -1e30)
        row_top = jnp.max(scores, axis=(2, 3), keepdims=True)
        weights = jnp.where(live_mask, jnp.exp(scores - row_top), 0.0)
        attn_probs = weights / jnp.sum(weights, axis=(2, 3), keepdims=True)
        probs_low = attn_probs.astype(jnp.bfloat16)
        attn_out = jnp.einsum(
            "gqjk,gjkd->gqd", probs_low, value_sets, preferred_element_type=jnp.float32
        )
        row_delta = jnp.sum(grad_group.astype(jnp.float32) * attn_out, axis=-1)
        prob_grad = jnp.einsum(
            "gqd,gjkd->gqjk", grad_group, value_sets, preferred_element_type=jnp.float32
        )
        score_low = (attn_probs * (prob_grad - row_delta[:, :, None, None])).astype(jnp.bfloat16)
        query_part = (
            jnp.einsum("gqjk,gjkd->gqd", score_low, key_sets, preferred_element_type=jnp.float32)
            * score_scale
        )
        key_parts = jnp.einsum(
            "gqjk,gqd->gjkd", score_low, query_group, preferred_element_type=jnp.float32
        )
        value_parts = jnp.einsum(
            "gqjk,gqd->gjkd", probs_low, grad_group, preferred_element_type=jnp.float32
        )
        key_sum = key_sum.at[lists_group].add(key_parts)
        value_sum = value_sum.at[lists_group].add(value_parts)
        return ((key_sum, value_sum), query_part.astype(jnp.bfloat16))

    def grouped(array):
        return array.reshape((nblocks // group, group) + array.shape[1:])

    empty_sum = jnp.zeros(query_blocks.shape, jnp.float32)
    final_state, query_part = lax.scan(
        scan_step,
        (empty_sum, empty_sum),
        (grouped(query_blocks), grouped(grad_blocks), grouped(lists_head), grouped(counts_head)),
    )
    key_sum, value_sum = final_state
    return (
        query_part.reshape(query_blocks.shape),
        (key_sum * score_scale).astype(jnp.bfloat16),
        value_sum.astype(jnp.bfloat16),
    )


def local(queries, key_states, value_states, grad_out, out_weight, block_lists, block_counts):
    tok_rows = queries.shape[1]
    model_width = queries.shape[2]
    head_total = model_width // HD
    head_local, nblocks, kslots = block_lists.shape

    def split_heads(matrix):
        return matrix.reshape(tok_rows, head_total, HD)

    def to_blocks(matrix):
        return jnp.moveaxis(matrix, 1, 0).reshape(head_local, nblocks, -1, HD)

    def from_blocks(blocks):
        return jnp.moveaxis(blocks.reshape(head_local, -1, HD), 0, 1)

    query_heads, key_heads, value_heads = (
        lax.all_to_all(split_heads(queries), "seq", split_axis=1, concat_axis=0, tiled=True),
        lax.all_to_all(split_heads(key_states), "seq", split_axis=1, concat_axis=0, tiled=True),
        lax.all_to_all(split_heads(value_states), "seq", split_axis=1, concat_axis=0, tiled=True),
    )
    query_blocks = to_blocks(query_heads)
    key_blocks = to_blocks(key_heads)
    value_blocks = to_blocks(value_heads)
    grad_rows = grad_out.reshape(tok_rows, model_width)
    attn_full = lax.dot_general(
        grad_rows,
        lax.all_gather(out_weight, "dp", axis=0, tiled=True),
        (((1,), (1,)), ((), ())),
        preferred_element_type=jnp.float32,
    )
    attn_low = attn_full.astype(jnp.bfloat16)
    grad_heads = lax.all_to_all(
        split_heads(attn_low), "seq", split_axis=1, concat_axis=0, tiled=True
    )
    grad_blocks = to_blocks(grad_heads)
    query_part, key_part, value_part = jax.vmap(whole_rows)(
        query_blocks, key_blocks, value_blocks, grad_blocks, block_lists, block_counts
    )
    returned = (
        lax.all_to_all(from_blocks(query_part), "seq", split_axis=0, concat_axis=1, tiled=True),
        lax.all_to_all(from_blocks(key_part), "seq", split_axis=0, concat_axis=1, tiled=True),
        lax.all_to_all(from_blocks(value_part), "seq", split_axis=0, concat_axis=1, tiled=True),
    )
    return (
        returned[0].reshape(1, tok_rows, model_width),
        returned[1].reshape(1, tok_rows, model_width),
        returned[2].reshape(1, tok_rows, model_width),
    )


def solution(mesh):
    placed = (
        P("dp", "seq", None),
        P("dp", "seq", None),
        P("dp", "seq", None),
        P("dp", "seq", None),
        P("dp", None),
        P("seq", None, None),
        P("seq", None),
    )
    return jax.shard_map(
        local,
        mesh=mesh,
        in_specs=placed,
        out_specs=(P("dp", "seq", None), P("dp", "seq", None), P("dp", "seq", None)),
        check_vma=False,
    )
```

profile of v0, /device:TPU:32, one launch (start us, length us, event | category | flops | bytes accessed | tf_op | source)
XLA Modules:
  0.0 279.4 jit_solution(4677492128257543968)
XLA Ops:
  10.0 7.1 %all-to-all-start = ((bf16[128,16,128]{2,0,1:T(8,128)(2,1)}), bf16[128,16,128]{2,0,1:T(8,128)(2,1)}, u32[]{:S(2)}, u32[]{:S(2)}) async-start(bf16[128,16,128]{2,0,1:T(8,128)(2,1)} %copy.81), calls=%async_computation | async-start | bytes 1048576 | tf_op jit(solution)/shard_map/all_to_all | solution.py:86
  18.1 10.6 %all-to-all-done = bf16[128,16,128]{2,0,1:T(8,128)(2,1)} async-done(((bf16[128,16,128]{2,0,1:T(8,128)(2,1)}), bf16[128,16,128]{2,0,1:T(8,128)(2,1)}, u32[]{:S(2)}, u32[]{:S(2)}) %all-to-all-start) | async-done | bytes 524320 | tf_op jit(solution)/shard_map/all_to_all | solution.py:86
  28.7 3.6 %all-to-all-start.1 = ((bf16[128,16,128]{0,2,1:T(8,128)(2,1)}), bf16[128,16,128]{0,2,1:T(8,128)(2,1)S(1)}, u32[]{:S(2)}, u32[]{:S(2)}) async-start(bf16[128,16,128]{0,2,1:T(8,128)(2,1)} %bitcast.29), calls=%async_computation.1 | async-start | bytes 1048576 | tf_op jit(solution)/shard_map/all_to_all | solution.py:87
  33.3 9.4 %all-to-all-done.1 = bf16[128,16,128]{0,2,1:T(8,128)(2,1)S(1)} async-done(((bf16[128,16,128]{0,2,1:T(8,128)(2,1)}), bf16[128,16,128]{0,2,1:T(8,128)(2,1)S(1)}, u32[]{:S(2)}, u32[]{:S(2)}) %all-to-all-start.1) | async-done | bytes 524320 | tf_op jit(solution)/shard_map/all_to_all | solution.py:87
  42.7 3.6 %all-to-all-start.3 = ((bf16[128,16,128]{0,2,1:T(8,128)(2,1)}), bf16[128,16,128]{0,2,1:T(8,128)(2,1)S(1)}, u32[]{:S(2)}, u32[]{:S(2)}) async-start(bf16[128,16,128]{0,2,1:T(8,128)(2,1)} %bitcast.38), calls=%async_computation.3 | async-start | bytes 1048576 | tf_op jit(solution)/shard_map/all_to_all | solution.py:88
  46.3 46.6 %all-gather.2.cloned.1.call-done = bf16[2048,2048]{1,0:T(8,128)(2,1)} async-done(((bf16[64,2048]{1,0:T(8,128)(2,1)}), bf16[2048,2048]{1,0:T(8,128)(2,1)}) %all-gather.2.cloned.1.call-update) | async-done | bytes 8388624 | tf_op jit(solution)/shard_map/all_gather | solution.py:96
  92.9 6.3 %fusion.29 = bf16[16,16,8,128]{3,2,1,0:T(8,128)(2,1)S(1)} fusion(bf16[2048,2048]{1,0:T(8,128)(2,1)} %all-gather.2.cloned.1.call-done, bf16[1,128,2048]{2,1,0:T(8,128)(2,1)S(1)} %copy-done), kind=kOutput, calls=%fused_computation.43 | convolution fusion | flops 1074003968 | bytes 9437184 | tf_op jit(solution)/shard_map/dot_general | solution.py:94
  100.1 6.9 %all-to-all-start.2 = ((bf16[128,16,128]{2,0,1:T(8,128)(2,1)}), bf16[128,16,128]{2,0,1:T(8,128)(2,1)}, u32[]{:S(2)}, u32[]{:S(2)}) async-start(bf16[128,16,128]{2,0,1:T(8,128)(2,1)} %bitcast.120), calls=%async_computation.2 | async-start | bytes 1048576 | tf_op jit(solution)/shard_map/all_to_all | solution.py:101
  109.7 9.3 %all-to-all-done.2 = bf16[128,16,128]{2,0,1:T(8,128)(2,1)} async-done(((bf16[128,16,128]{2,0,1:T(8,128)(2,1)}), bf16[128,16,128]{2,0,1:T(8,128)(2,1)}, u32[]{:S(2)}, u32[]{:S(2)}) %all-to-all-start.2) | async-done | bytes 524320 | tf_op jit(solution)/shard_map/all_to_all | solution.py:101
  121.2 104.3 %while.14 = (s32[]{:T(128)}, f32[1,16,128,128]{3,2,1,0:T(8,128)}, f32[1,16,128,128]{3,2,1,0:T(8,128)}, bf16[4,1,4,128,128]{4,3,2,1,0:T(8,128)(2,1)}, s32[4,1,4,8...) while((s32[]{:T(128)}, f32[1,16,128,128]{3,2,1,0:T(8,128)}, ...), condition=%wide.region_6.7_spmd, body=%wide.region_0.6_spmd.sunk | while | flops 821361536 | bytes 47997756 | solution.py:57
  133.4 6.1 %scatter_fusion.1 = f32[16,128,128]{2,1,0:T(8,128)} fusion(f32[16,128,128]{2,1,0:T(8,128)} %bitcast.168, s32[32]{0:T(128)S(1)} %reshape.276, f32[32,128,128]{2,1,0:T(8,128)S(1)} %bitcast.174), kind=kCustom, calls=%fused_computation.3.clone.1 | custom fusion | flops 524288 | bytes 6291584 | tf_op jit(solution)/shard_map/vmap()/while/body/eval_jaxpr/scatter-add | solution.py:50
  141.2 6.1 %scatter_fusion = f32[16,128,128]{2,1,0:T(8,128)} fusion(f32[16,128,128]{2,1,0:T(8,128)} %bitcast.163, s32[32]{0:T(128)S(1)} %reshape.276, f32[32,128,128]{2,1,0:T(8,128)S(1)} %bitcast.173), kind=kCustom, calls=%fused_computation.2.clone.1 | custom fusion | flops 524288 | bytes 6291584 | tf_op jit(solution)/shard_map/vmap()/while/body/eval_jaxpr/scatter-add | solution.py:49
  159.5 6.1 %scatter_fusion.1 = f32[16,128,128]{2,1,0:T(8,128)} fusion(f32[16,128,128]{2,1,0:T(8,128)} %bitcast.168, s32[32]{0:T(128)S(1)} %reshape.276, f32[32,128,128]{2,1,0:T(8,128)S(1)} %bitcast.174), kind=kCustom, calls=%fused_computation.3.clone.1 | custom fusion | flops 524288 | bytes 6291584 | tf_op jit(solution)/shard_map/vmap()/while/body/eval_jaxpr/scatter-add | solution.py:50
  167.3 6.1 %scatter_fusion = f32[16,128,128]{2,1,0:T(8,128)} fusion(f32[16,128,128]{2,1,0:T(8,128)} %bitcast.163, s32[32]{0:T(128)S(1)} %reshape.276, f32[32,128,128]{2,1,0:T(8,128)S(1)} %bitcast.173), kind=kCustom, calls=%fused_computation.2.clone.1 | custom fusion | flops 524288 | bytes 6291584 | tf_op jit(solution)/shard_map/vmap()/while/body/eval_jaxpr/scatter-add | solution.py:49
  185.6 6.2 %scatter_fusion.1 = f32[16,128,128]{2,1,0:T(8,128)} fusion(f32[16,128,128]{2,1,0:T(8,128)} %bitcast.168, s32[32]{0:T(128)S(1)} %reshape.276, f32[32,128,128]{2,1,0:T(8,128)S(1)} %bitcast.174), kind=kCustom, calls=%fused_computation.3.clone.1 | custom fusion | flops 524288 | bytes 6291584 | tf_op jit(solution)/shard_map/vmap()/while/body/eval_jaxpr/scatter-add | solution.py:50
  193.4 6.1 %scatter_fusion = f32[16,128,128]{2,1,0:T(8,128)} fusion(f32[16,128,128]{2,1,0:T(8,128)} %bitcast.163, s32[32]{0:T(128)S(1)} %reshape.276, f32[32,128,128]{2,1,0:T(8,128)S(1)} %bitcast.173), kind=kCustom, calls=%fused_computation.2.clone.1 | custom fusion | flops 524288 | bytes 6291584 | tf_op jit(solution)/shard_map/vmap()/while/body/eval_jaxpr/scatter-add | solution.py:49
  211.6 6.1 %scatter_fusion.1 = f32[16,128,128]{2,1,0:T(8,128)} fusion(f32[16,128,128]{2,1,0:T(8,128)} %bitcast.168, s32[32]{0:T(128)S(1)} %reshape.276, f32[32,128,128]{2,1,0:T(8,128)S(1)} %bitcast.174), kind=kCustom, calls=%fused_computation.3.clone.1 | custom fusion | flops 524288 | bytes 6291584 | tf_op jit(solution)/shard_map/vmap()/while/body/eval_jaxpr/scatter-add | solution.py:50
  219.4 6.1 %scatter_fusion = f32[16,128,128]{2,1,0:T(8,128)} fusion(f32[16,128,128]{2,1,0:T(8,128)} %bitcast.163, s32[32]{0:T(128)S(1)} %reshape.276, f32[32,128,128]{2,1,0:T(8,128)S(1)} %bitcast.173), kind=kCustom, calls=%fused_computation.2.clone.1 | custom fusion | flops 524288 | bytes 6291584 | tf_op jit(solution)/shard_map/vmap()/while/body/eval_jaxpr/scatter-add | solution.py:49
  229.0 3.8 %all-to-all-start.4 = ((bf16[16,2,8192]{2,1,0:T(2,128)(2,1)}), bf16[16,2,8192]{2,1,0:T(2,128)(2,1)S(1)}, u32[]{:S(2)}, u32[]{:S(2)}) async-start(bf16[16,2,8192]{2,1,0:T(2,128)(2,1)} %reshape.252), calls=%async_computation.4 | async-start | bytes 1048576 | tf_op jit(solution)/shard_map/all_to_all | solution.py:109
  236.1 7.3 %all-to-all-done.4 = bf16[16,2,8192]{2,1,0:T(2,128)(2,1)S(1)} async-done(((bf16[16,2,8192]{2,1,0:T(2,128)(2,1)}), bf16[16,2,8192]{2,1,0:T(2,128)(2,1)S(1)}, u32[]{:S(2)}, u32[]{:S(2)}) %all-to-all-start.4) | async-done | bytes 524320 | tf_op jit(solution)/shard_map/all_to_all | solution.py:109
  243.3 3.6 %all-to-all-start.5 = ((bf16[16,2,8192]{2,1,0:T(2,128)(2,1)}), bf16[16,2,8192]{2,1,0:T(2,128)(2,1)S(1)}, u32[]{:S(2)}, u32[]{:S(2)}) async-start(bf16[16,2,8192]{2,1,0:T(2,128)(2,1)} %reshape.254), calls=%async_computation.5 | async-start | bytes 1048576 | tf_op jit(solution)/shard_map/all_to_all | solution.py:110
  250.2 6.8 %all-to-all-done.5 = bf16[16,2,8192]{2,1,0:T(2,128)(2,1)S(1)} async-done(((bf16[16,2,8192]{2,1,0:T(2,128)(2,1)}), bf16[16,2,8192]{2,1,0:T(2,128)(2,1)S(1)}, u32[]{:S(2)}, u32[]{:S(2)}) %all-to-all-start.5) | async-done | bytes 524320 | tf_op jit(solution)/shard_map/all_to_all | solution.py:110
  257.0 3.6 %all-to-all-start.6 = ((bf16[16,2,8192]{2,1,0:T(2,128)(2,1)}), bf16[16,2,8192]{2,1,0:T(2,128)(2,1)S(1)}, u32[]{:S(2)}, u32[]{:S(2)}) async-start(bf16[16,2,8192]{2,1,0:T(2,128)(2,1)} %reshape.256), calls=%async_computation.6 | async-start | bytes 1048576 | tf_op jit(solution)/shard_map/all_to_all | solution.py:111
  264.4 6.3 %all-to-all-done.6 = bf16[16,2,8192]{2,1,0:T(2,128)(2,1)S(1)} async-done(((bf16[16,2,8192]{2,1,0:T(2,128)(2,1)}), bf16[16,2,8192]{2,1,0:T(2,128)(2,1)S(1)}, u32[]{:S(2)}, u32[]{:S(2)}) %all-to-all-start.6) | async-done | bytes 524320 | tf_op jit(solution)/shard_map/all_to_all | solution.py:111
  (128 shorter events, 81.5 us)
Async XLA Ops:
  7.2 85.7 %copy-start = (bf16[1,128,2048]{2,1,0:T(8,128)(2,1)S(1)}, bf16[1,128,2048]{2,1,0:T(8,128)(2,1)}, u32[]{:S(2)}) copy-start(bf16[1,128,2048]{2,1,0:T(8,128)(2,1)} %param.12) | copy-start | bytes 1572868
  7.2 9.9 %copy-start.3 = (bf16[1,128,2048]{2,1,0:T(8,128)(2,1)S(1)}, bf16[1,128,2048]{2,1,0:T(8,128)(2,1)}, u32[]{:S(2)}) copy-start(bf16[1,128,2048]{2,1,0:T(8,128)(2,1)} %param.10) | copy-start | bytes 1572868
  7.2 85.7 %all-gather.2.cloned.1.call-start = ((), (), s32[]{:S(2)}) async-start(), calls=%async_computation.7 | async-start | bytes 8650752 | tf_op jit(solution)/shard_map/all_gather | solution.py:96
  9.1 23.2 %copy-start.4 = (bf16[1,128,2048]{2,1,0:T(8,128)(2,1)S(1)}, bf16[1,128,2048]{2,1,0:T(8,128)(2,1)}, u32[]{:S(2)}) copy-start(bf16[1,128,2048]{2,1,0:T(8,128)(2,1)} %param.11) | copy-start | bytes 1572868
  10.0 18.7 %all-to-all-start = ((bf16[128,16,128]{2,0,1:T(8,128)(2,1)}), bf16[128,16,128]{2,0,1:T(8,128)(2,1)}, u32[]{:S(2)}, u32[]{:S(2)}) async-start(bf16[128,16,128]{2,0,1:T(8,128)(2,1)} %copy.81), calls=%async_computation | async-start | bytes 1048576 | tf_op jit(solution)/shard_map/all_to_all | solution.py:86
  28.7 14.0 %all-to-all-start.1 = ((bf16[128,16,128]{0,2,1:T(8,128)(2,1)}), bf16[128,16,128]{0,2,1:T(8,128)(2,1)S(1)}, u32[]{:S(2)}, u32[]{:S(2)}) async-start(bf16[128,16,128]{0,2,1:T(8,128)(2,1)} %bitcast.29), calls=%async_computation.1 | async-start | bytes 1048576 | tf_op jit(solution)/shard_map/all_to_all | solution.py:87
  42.7 57.4 %all-to-all-start.3 = ((bf16[128,16,128]{0,2,1:T(8,128)(2,1)}), bf16[128,16,128]{0,2,1:T(8,128)(2,1)S(1)}, u32[]{:S(2)}, u32[]{:S(2)}) async-start(bf16[128,16,128]{0,2,1:T(8,128)(2,1)} %bitcast.38), calls=%async_computation.3 | async-start | bytes 1048576 | tf_op jit(solution)/shard_map/all_to_all | solution.py:88
  99.2 8.4 %copy-start.6 = (s32[1,16]{1,0:T(1,128)S(1)}, s32[1,16]{1,0:T(1,128)}, u32[]{:S(2)}) copy-start(s32[1,16]{1,0:T(1,128)} %param.15) | copy-start | bytes 196
  99.2 9.1 %copy-start.5 = (s32[1,16,8]{1,2,0:T(8,128)S(1)}, s32[1,16,8]{1,2,0:T(8,128)}, u32[]{:S(2)}) copy-start(s32[1,16,8]{1,2,0:T(8,128)} %param.14) | copy-start | bytes 1540
  100.1 18.9 %all-to-all-start.2 = ((bf16[128,16,128]{2,0,1:T(8,128)(2,1)}), bf16[128,16,128]{2,0,1:T(8,128)(2,1)}, u32[]{:S(2)}, u32[]{:S(2)}) async-start(bf16[128,16,128]{2,0,1:T(8,128)(2,1)} %bitcast.120), calls=%async_computation.2 | async-start | bytes 1048576 | tf_op jit(solution)/shard_map/all_to_all | solution.py:101
  125.0 2.1 copy-start.2
  130.6 2.8 %copy-start.1 = (bf16[4,128,8,128]{1,3,2,0:T(8,128)(2,1)}, bf16[4,128,8,128]{1,3,2,0:T(8,128)(2,1)S(1)}, u32[]{:S(2)}) copy-start(bf16[4,128,8,128]{1,3,2,0:T(8,128)(2,1)S(1)} %multiply_convert_fusion.3) | copy-start | bytes 3145732 | tf_op jit(solution)/shard_map/vmap()/while
  151.1 2.1 copy-start.2
  156.7 2.8 %copy-start.1 = (bf16[4,128,8,128]{1,3,2,0:T(8,128)(2,1)}, bf16[4,128,8,128]{1,3,2,0:T(8,128)(2,1)S(1)}, u32[]{:S(2)}) copy-start(bf16[4,128,8,128]{1,3,2,0:T(8,128)(2,1)S(1)} %multiply_convert_fusion.3) | copy-start | bytes 3145732 | tf_op jit(solution)/shard_map/vmap()/while
  177.1 2.1 copy-start.2
  182.8 2.8 %copy-start.1 = (bf16[4,128,8,128]{1,3,2,0:T(8,128)(2,1)}, bf16[4,128,8,128]{1,3,2,0:T(8,128)(2,1)S(1)}, u32[]{:S(2)}) copy-start(bf16[4,128,8,128]{1,3,2,0:T(8,128)(2,1)S(1)} %multiply_convert_fusion.3) | copy-start | bytes 3145732 | tf_op jit(solution)/shard_map/vmap()/while
  203.2 2.1 copy-start.2
  208.8 2.8 %copy-start.1 = (bf16[4,128,8,128]{1,3,2,0:T(8,128)(2,1)}, bf16[4,128,8,128]{1,3,2,0:T(8,128)(2,1)S(1)}, u32[]{:S(2)}) copy-start(bf16[4,128,8,128]{1,3,2,0:T(8,128)(2,1)S(1)} %multiply_convert_fusion.3) | copy-start | bytes 3145732 | tf_op jit(solution)/shard_map/vmap()/while
  229.0 14.4 %all-to-all-start.4 = ((bf16[16,2,8192]{2,1,0:T(2,128)(2,1)}), bf16[16,2,8192]{2,1,0:T(2,128)(2,1)S(1)}, u32[]{:S(2)}, u32[]{:S(2)}) async-start(bf16[16,2,8192]{2,1,0:T(2,128)(2,1)} %reshape.252), calls=%async_computation.4 | async-start | bytes 1048576 | tf_op jit(solution)/shard_map/all_to_all | solution.py:109
  243.3 13.7 %all-to-all-start.5 = ((bf16[16,2,8192]{2,1,0:T(2,128)(2,1)}), bf16[16,2,8192]{2,1,0:T(2,128)(2,1)S(1)}, u32[]{:S(2)}, u32[]{:S(2)}) async-start(bf16[16,2,8192]{2,1,0:T(2,128)(2,1)} %reshape.254), calls=%async_computation.5 | async-start | bytes 1048576 | tf_op jit(solution)/shard_map/all_to_all | solution.py:110
  257.0 13.7 %all-to-all-start.6 = ((bf16[16,2,8192]{2,1,0:T(2,128)(2,1)}), bf16[16,2,8192]{2,1,0:T(2,128)(2,1)S(1)}, u32[]{:S(2)}, u32[]{:S(2)}) async-start(bf16[16,2,8192]{2,1,0:T(2,128)(2,1)} %reshape.256), calls=%async_computation.6 | async-start | bytes 1048576 | tf_op jit(solution)/shard_map/all_to_all | solution.py:111
Sparse Core Ops, SparseCore 0:
  10.1 82.7 all-gather.1
where the time goes:
time: 282 us; the launch traced here: 279 us
  waiting for transfers between devices  97 us (34%)
  other arithmetic  59.2 us (21%)
  matrix products  43.9 us (16%)
  local copies, waits for them, and re-layouts  32.8 us (12%)
  starting transfers between devices  32.1 us (11%)
  between operations  14.3 us (5%)
    all_gather x1, waiting for transfers between devices, local(): lax.all_gather(out_weight, 'dp', axis=0, tiled=True)  46.6 us
    scatter-add x4, other arithmetic, scan_step(): value_sum = value_sum.at[lists_group].add(value_parts)  24.5 us
    scatter-add x8, other arithmetic, scan_step(): key_sum = key_sum.at[lists_group].add(key_parts)  24.4 us
    unnamed x27, local copies, waits for them, and re-layouts  11.3 us
    gather x4, local copies, waits for them, and re-layouts, scan_step(): value_sets = value_blocks[lists_group]  10.9 us
    all_to_all x1, waiting for transfers between devices, local(): lax.all_to_all(split_heads(queries), 'seq', split_axis=1, concat_axis=0,...  10.6 us
    all_to_all x1, waiting for transfers between devices, local(): lax.all_to_all(split_heads(key_states), 'seq', split_axis=1, concat_axis=...  9.42 us
    all_to_all x1, waiting for transfers between devices, local(): lax.all_to_all(split_heads(attn_low), 'seq', split_axis=1, concat_axis=0,...  9.34 us
  transfers between devices with their start and end apart: 8, of which 7 were waited for; matrix products, arithmetic and copies ran while one was open for 9% of the time, Pallas kernels for 0%

commit v1 on v0

--- a/solution.py
+++ b/solution.py
@@ -68,6 +68,15 @@
 
 
 def local(queries, key_states, value_states, grad_out, out_weight, block_lists, block_counts):
+
+    def _save_zones(xs, row_dim):
+        runs = []
+        for _ in range(lax.axis_size("dp")):
+            runs.append(xs)
+        return jnp.concatenate(
+            lax.all_to_all(jnp.stack(runs), axis_name="dp", split_axis=0, concat_axis=0), row_dim
+        )
+
     tok_rows = queries.shape[1]
     model_width = queries.shape[2]
     head_total = model_width // HD
@@ -93,7 +102,7 @@
     grad_rows = grad_out.reshape(tok_rows, model_width)
     attn_full = lax.dot_general(
         grad_rows,
-        lax.all_gather(out_weight, "dp", axis=0, tiled=True),
+        _save_zones(out_weight, 0),
         (((1,), (1,)), ((), ())),
         preferred_element_type=jnp.float32,
     )

time: 282 us -> 625 us (2.22)
  waiting for transfers between devices: 97 us -> 414 us
  matrix products: 43.9 us -> 63.4 us
  blocking collectives: 0 us -> 13.7 us
  between operations: 14.3 us -> 0.9 us
  starting transfers between devices: 32.1 us -> 41.3 us
    all_to_all x1, waiting for transfers between devices: 9.42 us -> 369 us  [_save_zones(): lax.all_to_all(jnp.stack(runs), axis_name='dp', split_axis=0, concat_axis=0)]
    all_gather x1 -> x0, waiting for transfers between devices: 46.6 us -> none  [local(): lax.all_gather(out_weight, 'dp', axis=0, tiled=True)]
    all_to_all x0 -> x1, blocking collectives: none -> 13.7 us  [local(): lax.all_to_all(split_heads(key_states), 'seq', split_axis=1, concat_axis=...]
    all_to_all x1, starting transfers between devices: 3.57 us -> 15.5 us  [_save_zones(): lax.all_to_all(jnp.stack(runs), axis_name='dp', split_axis=0, concat_axis=0)]
  transfers between devices with their start and end apart: 8 -> 7, of which waited for: 7 -> 7; matrix products, arithmetic and copies ran while one was open for 9% -> 3% of each run, Pallas kernels for 0% -> 0%
where the time goes in v1:
time: 625 us; the launch traced here: 623 us
  waiting for transfers between devices  414 us (66%)
  matrix products  63.4 us (10%)
  other arithmetic  54.3 us (9%)
  starting transfers between devices  41.3 us (7%)
  local copies, waits for them, and re-layouts  35.4 us (6%)
  blocking collectives  13.7 us (2%)
    all_to_all x1, waiting for transfers between devices, _save_zones(): lax.all_to_all(jnp.stack(runs), axis_name='dp', split_axis=0, concat_axis=0)  369 us
    scatter-add x4, other arithmetic, scan_step(): value_sum = value_sum.at[lists_group].add(value_parts)  27.9 us
    scatter-add x8, other arithmetic, scan_step(): key_sum = key_sum.at[lists_group].add(key_parts)  18.7 us
    all_to_all x1, starting transfers between devices, _save_zones(): lax.all_to_all(jnp.stack(runs), axis_name='dp', split_axis=0, concat_axis=0)  15.5 us
    all_to_all x1, blocking collectives, local(): lax.all_to_all(split_heads(key_states), 'seq', split_axis=1, concat_axis=...  13.7 us
  transfers between devices with their start and end apart: 7, of which 7 were waited for; matrix products, arithmetic and copies ran while one was open for 3% of the time, Pallas kernels for 0%

profile of v1, /device:TPU:32, one launch (start us, length us, event | category | flops | bytes accessed | tf_op | source)
XLA Modules:
  0.0 622.9 jit_solution(9810895889124533939)
XLA Ops:
  2.8 7.0 %all-to-all-start = ((bf16[128,16,128]{2,0,1:T(8,128)(2,1)}), bf16[128,16,128]{2,0,1:T(8,128)(2,1)S(1)}, u32[]{:S(2)}, u32[]{:S(2)}) async-start(bf16[128,16,128]{2,0,1:T(8,128)(2,1)} %copy.81), calls=%async_computation | async-start | bytes 1048576 | tf_op jit(solution)/shard_map/all_to_all | solution.py:95
  10.2 11.2 %all-to-all-done = bf16[128,16,128]{2,0,1:T(8,128)(2,1)S(1)} async-done(((bf16[128,16,128]{2,0,1:T(8,128)(2,1)}), bf16[128,16,128]{2,0,1:T(8,128)(2,1)S(1)}, u32[]{:S(2)}, u32[]{:S(2)}) %all-to-all-start) | async-done | bytes 524320 | tf_op jit(solution)/shard_map/all_to_all | solution.py:95
  21.4 13.7 %all_to_all.110 = bf16[128,16,128]{0,2,1:T(8,128)(2,1)S(1)} all-to-all(bf16[128,16,128]{0,2,1:T(8,128)(2,1)S(1)} %bitcast.190), channel_id=1, replica_groups=mesh['seq'=16,'dp'=32] {'seq'}, dimensions={1} | all-to-all | bytes 1048576 | tf_op jit(solution)/shard_map/all_to_all | solution.py:96
  35.1 4.3 stack.2
  39.4 15.5 %all-to-all-start.2 = ((bf16[32,64,2048]{2,1,0:T(8,128)(2,1)}), bf16[32,64,2048]{2,1,0:T(8,128)(2,1)}, u32[]{:S(2)}, u32[]{:S(2)}) async-start(bf16[32,64,2048]{2,1,0:T(8,128)(2,1)} %stack.2), calls=%async_computation.2 | async-start | bytes 16777216 | tf_op jit(solution)/shard_map/all_to_all | solution.py:77
  56.0 368.9 %all-to-all-done.2 = bf16[32,64,2048]{2,1,0:T(8,128)(2,1)} async-done(((bf16[32,64,2048]{2,1,0:T(8,128)(2,1)}), bf16[32,64,2048]{2,1,0:T(8,128)(2,1)}, u32[]{:S(2)}, u32[]{:S(2)}) %all-to-all-start.2) | async-done | bytes 8388640 | tf_op jit(solution)/shard_map/all_to_all | solution.py:77
  424.9 3.6 all-to-all-start.4
  428.5 6.3 %fusion.29 = bf16[16,16,8,128]{3,2,1,0:T(8,128)(2,1)S(1)} fusion(bf16[2048,2048]{1,0:T(8,128)(2,1)} %bitcast.34, bf16[1,128,2048]{2,1,0:T(8,128)(2,1)S(1)} %copy-done), kind=kOutput, calls=%fused_computation.43 | convolution fusion | flops 1074003968 | bytes 9437184 | tf_op jit(solution)/shard_map/dot_general | solution.py:103
  435.7 4.2 all-to-all-done.4
  439.9 4.4 all-to-all-start.3
  447.0 7.7 %all-to-all-done.3 = bf16[128,16,128]{2,0,1:T(8,128)(2,1)} async-done(((bf16[128,16,128]{2,0,1:T(8,128)(2,1)}), bf16[128,16,128]{2,0,1:T(8,128)(2,1)}, u32[]{:S(2)}, u32[]{:S(2)}) %all-to-all-start.3) | async-done | bytes 524320 | tf_op jit(solution)/shard_map/all_to_all | solution.py:110
  455.9 121.5 %while.14 = (s32[]{:T(128)}, f32[1,16,128,128]{3,2,1,0:T(8,128)S(1)}, f32[1,16,128,128]{3,2,1,0:T(8,128)}, bf16[4,1,4,128,128]{4,3,2,1,0:T(8,128)(2,1)}, s32[4,1...) while((s32[]{:T(128)}, ...), condition=%wide.region_6.7_spmd, body=%wide.region_0.6_spmd.sunk | while | flops 821361536 | bytes 64777560 | solution.py:57
  461.9 7.0 %scatter_fusion.1 = f32[16,128,128]{2,1,0:T(8,128)} fusion(f32[16,128,128]{2,1,0:T(8,128)} %bitcast.177, s32[32]{0:T(128)S(1)} %reshape.282, f32[32,128,128]{2,1,0:T(8,128)} %bitcast.179), kind=kCustom, calls=%fused_computation.3.clone.1 | custom fusion | flops 524288 | bytes 6291584 | tf_op jit(solution)/shard_map/vmap()/while/body/eval_jaxpr/scatter-add | solution.py:50
  479.2 4.7 scatter_fusion
  492.3 7.0 %scatter_fusion.1 = f32[16,128,128]{2,1,0:T(8,128)} fusion(f32[16,128,128]{2,1,0:T(8,128)} %bitcast.177, s32[32]{0:T(128)S(1)} %reshape.282, f32[32,128,128]{2,1,0:T(8,128)} %bitcast.179), kind=kCustom, calls=%fused_computation.3.clone.1 | custom fusion | flops 524288 | bytes 6291584 | tf_op jit(solution)/shard_map/vmap()/while/body/eval_jaxpr/scatter-add | solution.py:50
  509.6 4.7 scatter_fusion
  522.7 7.0 %scatter_fusion.1 = f32[16,128,128]{2,1,0:T(8,128)} fusion(f32[16,128,128]{2,1,0:T(8,128)} %bitcast.177, s32[32]{0:T(128)S(1)} %reshape.282, f32[32,128,128]{2,1,0:T(8,128)} %bitcast.179), kind=kCustom, calls=%fused_computation.3.clone.1 | custom fusion | flops 524288 | bytes 6291584 | tf_op jit(solution)/shard_map/vmap()/while/body/eval_jaxpr/scatter-add | solution.py:50
  539.9 4.7 scatter_fusion
  553.0 7.0 %scatter_fusion.1 = f32[16,128,128]{2,1,0:T(8,128)} fusion(f32[16,128,128]{2,1,0:T(8,128)} %bitcast.177, s32[32]{0:T(128)S(1)} %reshape.282, f32[32,128,128]{2,1,0:T(8,128)} %bitcast.179), kind=kCustom, calls=%fused_computation.3.clone.1 | custom fusion | flops 524288 | bytes 6291584 | tf_op jit(solution)/shard_map/vmap()/while/body/eval_jaxpr/scatter-add | solution.py:50
  570.3 4.7 scatter_fusion
  585.6 8.1 %all-to-all-done.6 = bf16[16,2,8192]{2,1,0:T(2,128)(2,1)S(1)} async-done(((bf16[16,2,8192]{2,1,0:T(2,128)(2,1)}), bf16[16,2,8192]{2,1,0:T(2,128)(2,1)S(1)}, u32[]{:S(2)}, u32[]{:S(2)}) %all-to-all-start.6) | async-done | bytes 524320 | tf_op jit(solution)/shard_map/all_to_all | solution.py:119
  600.2 7.1 %all-to-all-done.7 = bf16[16,2,8192]{2,1,0:T(2,128)(2,1)S(1)} async-done(((bf16[16,2,8192]{2,1,0:T(2,128)(2,1)}), bf16[16,2,8192]{2,1,0:T(2,128)(2,1)S(1)}, u32[]{:S(2)}, u32[]{:S(2)}) %all-to-all-start.7) | async-done | bytes 524320 | tf_op jit(solution)/shard_map/all_to_all | solution.py:120
  607.3 3.6 all-to-all-start.5
  614.7 6.3 %all-to-all-done.5 = bf16[16,2,8192]{2,1,0:T(2,128)(2,1)S(1)} async-done(((bf16[16,2,8192]{2,1,0:T(2,128)(2,1)}), bf16[16,2,8192]{2,1,0:T(2,128)(2,1)S(1)}, u32[]{:S(2)}, u32[]{:S(2)}) %all-to-all-start.5) | async-done | bytes 524320 | tf_op jit(solution)/shard_map/all_to_all | solution.py:118
  (149 shorter events, 103.2 us)
Async XLA Ops:
  0.6 427.8 %copy-start = (bf16[1,128,2048]{2,1,0:T(8,128)(2,1)S(1)}, bf16[1,128,2048]{2,1,0:T(8,128)(2,1)}, u32[]{:S(2)}) copy-start(bf16[1,128,2048]{2,1,0:T(8,128)(2,1)} %param.12) | copy-start | bytes 1572868
  0.6 9.2 %copy-start.7 = (bf16[1,128,2048]{2,1,0:T(8,128)(2,1)S(1)}, bf16[1,128,2048]{2,1,0:T(8,128)(2,1)}, u32[]{:S(2)}) copy-start(bf16[1,128,2048]{2,1,0:T(8,128)(2,1)} %param.10) | copy-start | bytes 1572868
  1.9 33.2 %copy-start.9 = (bf16[64,2048]{1,0:T(8,128)(2,1)S(1)}, bf16[64,2048]{1,0:T(8,128)(2,1)}, u32[]{:S(2)}) copy-start(bf16[64,2048]{1,0:T(8,128)(2,1)} %param.13) | copy-start | bytes 786436
  2.8 18.6 %all-to-all-start = ((bf16[128,16,128]{2,0,1:T(8,128)(2,1)}), bf16[128,16,128]{2,0,1:T(8,128)(2,1)S(1)}, u32[]{:S(2)}, u32[]{:S(2)}) async-start(bf16[128,16,128]{2,0,1:T(8,128)(2,1)} %copy.81), calls=%async_computation | async-start | bytes 1048576 | tf_op jit(solution)/shard_map/all_to_all | solution.py:95
  21.4 18.0 %copy-start.6 = (bf16[128,16,128]{2,0,1:T(8,128)(2,1)}, bf16[128,16,128]{2,0,1:T(8,128)(2,1)S(1)}, u32[]{:S(2)}) copy-start(bf16[128,16,128]{2,0,1:T(8,128)(2,1)S(1)} %all-to-all-done) | copy-start | bytes 1572868
  39.4 15.6 %copy-start.8 = (bf16[1,128,2048]{2,1,0:T(8,128)(2,1)S(1)}, bf16[1,128,2048]{2,1,0:T(8,128)(2,1)}, u32[]{:S(2)}) copy-start(bf16[1,128,2048]{2,1,0:T(8,128)(2,1)} %param.11) | copy-start | bytes 1572868
  39.4 385.5 %all-to-all-start.2 = ((bf16[32,64,2048]{2,1,0:T(8,128)(2,1)}), bf16[32,64,2048]{2,1,0:T(8,128)(2,1)}, u32[]{:S(2)}, u32[]{:S(2)}) async-start(bf16[32,64,2048]{2,1,0:T(8,128)(2,1)} %stack.2), calls=%async_computation.2 | async-start | bytes 16777216 | tf_op jit(solution)/shard_map/all_to_all | solution.py:77
  424.9 15.1 %all-to-all-start.4 = ((bf16[128,16,128]{0,2,1:T(8,128)(2,1)}), bf16[128,16,128]{0,2,1:T(8,128)(2,1)S(1)}, u32[]{:S(2)}, u32[]{:S(2)}) async-start(bf16[128,16,128]{0,2,1:T(8,128)(2,1)} %bitcast.39), calls=%async_computation.4 | async-start | bytes 1048576 | tf_op jit(solution)/shard_map/all_to_all | solution.py:97
  434.8 10.2 %copy-start.11 = (s32[1,16]{1,0:T(1,128)S(1)}, s32[1,16]{1,0:T(1,128)}, u32[]{:S(2)}) copy-start(s32[1,16]{1,0:T(1,128)} %param.15) | copy-start | bytes 196
  434.8 10.8 %copy-start.10 = (s32[1,16,8]{1,2,0:T(8,128)S(1)}, s32[1,16,8]{1,2,0:T(8,128)}, u32[]{:S(2)}) copy-start(s32[1,16,8]{1,2,0:T(8,128)} %param.14) | copy-start | bytes 1540
  439.9 14.7 %all-to-all-start.3 = ((bf16[128,16,128]{2,0,1:T(8,128)(2,1)}), bf16[128,16,128]{2,0,1:T(8,128)(2,1)}, u32[]{:S(2)}, u32[]{:S(2)}) async-start(bf16[128,16,128]{2,0,1:T(8,128)(2,1)} %bitcast.121), calls=%async_computation.3 | async-start | bytes 1048576 | tf_op jit(solution)/shard_map/all_to_all | solution.py:110
  458.2 3.7 copy-start.1
  471.7 3.0 copy-start.5
  488.6 3.7 copy-start.1
  502.0 3.0 copy-start.5
  518.9 3.7 copy-start.1
  532.4 3.0 copy-start.2
  532.4 3.0 copy-start.5
  549.3 3.7 copy-start.1
  562.7 3.0 copy-start.5
  577.3 6.2 copy-start.3
  579.9 13.7 %all-to-all-start.6 = ((bf16[16,2,8192]{2,1,0:T(2,128)(2,1)}), bf16[16,2,8192]{2,1,0:T(2,128)(2,1)S(1)}, u32[]{:S(2)}, u32[]{:S(2)}) async-start(bf16[16,2,8192]{2,1,0:T(2,128)(2,1)} %reshape.260), calls=%async_computation.6 | async-start | bytes 1048576 | tf_op jit(solution)/shard_map/all_to_all | solution.py:119
  593.6 13.7 %all-to-all-start.7 = ((bf16[16,2,8192]{2,1,0:T(2,128)(2,1)}), bf16[16,2,8192]{2,1,0:T(2,128)(2,1)S(1)}, u32[]{:S(2)}, u32[]{:S(2)}) async-start(bf16[16,2,8192]{2,1,0:T(2,128)(2,1)} %reshape.262), calls=%async_computation.7 | async-start | bytes 1048576 | tf_op jit(solution)/shard_map/all_to_all | solution.py:120
  607.3 13.7 %all-to-all-start.5 = ((bf16[16,2,8192]{2,1,0:T(2,128)(2,1)}), bf16[16,2,8192]{2,1,0:T(2,128)(2,1)S(1)}, u32[]{:S(2)}, u32[]{:S(2)}) async-start(bf16[16,2,8192]{2,1,0:T(2,128)(2,1)} %reshape.258), calls=%async_computation.5 | async-start | bytes 1048576 | tf_op jit(solution)/shard_map/all_to_all | solution.py:118
  (7 other events, 20.3 us)
